TPU v7x, 256 devices: a whole 4x4x8 slice. The times are simulated.
256 devices in a mesh: pipe: 4 (over x), seq: 64 (over y, z, core).
Axes of the slice: x: 4, y: 4, z: 8, core: 2. Of those that a mesh axis runs over, the one named last changes fastest.
Arguments:
- acts: bfloat16 [4, 16384, 1024], P('pipe', 'seq'), may hold values from -6 to 6
- cotan: bfloat16 [4, 16384, 1024], P('pipe', 'seq'), may hold values from -6 to 6
- proj_in: bfloat16 [4, 1024, 2048], P('pipe'), may hold values from -0.1875 to 0.1875
- proj_out: bfloat16 [4, 1024, 1024], P('pipe'), may hold values from -0.1875 to 0.1875
- block_mix: bfloat16 [4, 16384, 256], P('pipe', 'seq'), may hold values from -0.375 to 0.375
- twiddle: float32 [4, 6, 2, 2, 1024], P('pipe'), may hold values from -2.5 to 2.5
Outputs:
- mixed: bfloat16 [4, 16384, 1024], P('pipe', 'seq')
- grad_prev: bfloat16 [4, 16384, 1024], P('pipe', 'seq')
- grad_in_proj: float32 [4, 1024, 2048], P('pipe', 'seq')
- grad_out_proj: float32 [4, 1024, 1024], P('pipe', 'seq')
- grad_block_mix: float32 [4, 16384, 256], P('pipe', 'seq')
- grad_twiddle: float32 [4, 6, 2, 2, 1024], P('pipe')
All inputs are finite; a program needn't handle non-finite values.
Results may differ from a plain program's by a relative error of at most 0.014.
Values may be sent and summed in bfloat16 or wider, within the bound.
A program may use at most 128 MiB of HBM per device.

v0:
```python
import jax
import jax.numpy as jnp
from jax import lax
from jax.sharding import PartitionSpec as P


def swapped(block, axis, apart):
    count = lax.axis_size(axis)
    route = []
    for low in range(count):
        high = low | 1 << apart
        if high != low and high < count:
            route += [(low, high), (high, low)]
    return lax.ppermute(block, axis, route)


def from_behind(value, axis, steps):
    count = lax.axis_size(axis)
    first, last = (max(0, -steps), min(count, count - steps))
    return lax.ppermute(value, axis, [(source, source + steps) for source in range(first, last)])


def on_device(acts, cotan, proj_in, proj_out, block_mix, twiddle):
    inputs = acts[0]
    grad_out = cotan[0]
    w_in = proj_in[0]
    w_out = proj_out[0]
    square_mix = block_mix[0]
    twiddle_w = twiddle[0]
    row_count, feature_count = inputs.shape
    seq_count = lax.axis_size("seq")
    segment_total = seq_count.bit_length() - 1
    position = lax.axis_index("seq")
    projected = jnp.dot(inputs, w_in, preferred_element_type=jnp.float32)
    value = projected[:, :feature_count].astype(jnp.bfloat16)
    gate = projected[:, feature_count:].astype(jnp.bfloat16)
    first_segment = jnp.dot(square_mix, value, preferred_element_type=jnp.float32).astype(
        jnp.bfloat16
    )
    partials = [None] * segment_total
    stored = []
    current = first_segment
    for segment_bit in range(segment_total):
        partner = swapped(current, "seq", segment_bit)
        upper_half = position >> segment_bit & 1
        segment_coef = jnp.where(
            upper_half == 0, twiddle_w[segment_bit, 0], twiddle_w[segment_bit, 1]
        )
        stored.append((current, partner))
        current = (
            segment_coef[0] * current.astype(jnp.float32)
            + segment_coef[1] * partner.astype(jnp.float32)
        ).astype(jnp.bfloat16)
    hidden = (current.astype(jnp.float32) * gate.astype(jnp.float32)).astype(jnp.bfloat16)
    mixed_out = jnp.dot(hidden, w_out, preferred_element_type=jnp.float32).astype(jnp.bfloat16)
    d_hidden = lax.dot_general(
        grad_out, w_out, (((1,), (1,)), ((), ())), preferred_element_type=jnp.float32
    ).astype(jnp.bfloat16)
    wout_term = lax.dot_general(
        hidden, grad_out, (((0,), (0,)), ((), ())), preferred_element_type=jnp.float32
    )
    d_monarch = (d_hidden.astype(jnp.float32) * gate.astype(jnp.float32)).astype(jnp.bfloat16)
    d_gate = (d_hidden.astype(jnp.float32) * current.astype(jnp.float32)).astype(jnp.bfloat16)
    grad_now = d_monarch
    for segment_bit in range(segment_total - 1, -1, -1):
        grad_partner = swapped(grad_now, "seq", segment_bit)
        upper_half = position >> segment_bit & 1
        own_coef = jnp.where(upper_half == 0, twiddle_w[segment_bit, 0], twiddle_w[segment_bit, 1])
        peer_coef = jnp.where(upper_half == 0, twiddle_w[segment_bit, 1], twiddle_w[segment_bit, 0])
        saved_own, saved_peer = stored[segment_bit]
        grad_float = grad_now.astype(jnp.float32)
        own_row = jnp.stack(
            [
                jnp.sum(grad_float * saved_own.astype(jnp.float32), axis=0),
                jnp.sum(grad_float * saved_peer.astype(jnp.float32), axis=0),
            ]
        )
        empty_row = jnp.zeros_like(own_row)
        partials[segment_bit] = jnp.where(
            upper_half == 0, jnp.stack([own_row, empty_row]), jnp.stack([empty_row, own_row])
        )
        grad_now = (
            own_coef[0] * grad_float + peer_coef[1] * grad_partner.astype(jnp.float32)
        ).astype(jnp.bfloat16)
    twiddle_grad = lax.psum(jnp.stack(partials), "seq")
    d_value = lax.dot_general(
        square_mix, grad_now, (((0,), (0,)), ((), ())), preferred_element_type=jnp.float32
    ).astype(jnp.bfloat16)
    grad_square = lax.dot_general(
        grad_now, value, (((1,), (1,)), ((), ())), preferred_element_type=jnp.float32
    )
    d_projected = jnp.concatenate([d_value, d_gate], axis=1)
    win_term = lax.dot_general(
        inputs, d_projected, (((0,), (0,)), ((), ())), preferred_element_type=jnp.float32
    )
    win_share, wout_share = (
        lax.psum_scatter(win_term, "seq", scatter_dimension=0, tiled=True),
        lax.psum_scatter(wout_term, "seq", scatter_dimension=0, tiled=True),
    )
    input_grad = lax.dot_general(
        d_projected, w_in, (((1,), (1,)), ((), ())), preferred_element_type=jnp.float32
    ).astype(jnp.bfloat16)
    handed = from_behind(input_grad, "pipe", -1)
    return (
        mixed_out[None],
        handed[None],
        win_share[None],
        wout_share[None],
        grad_square[None],
        twiddle_grad[None],
    )


def solution(mesh):
    in_specs = (
        P("pipe", "seq", None),
        P("pipe", "seq", None),
        P("pipe", None, None),
        P("pipe", None, None),
        P("pipe", "seq", None),
        P("pipe", None, None, None, None),
    )
    out_specs = (
        P("pipe", "seq", None),
        P("pipe", "seq", None),
        P("pipe", "seq", None),
        P("pipe", "seq", None),
        P("pipe", "seq", None),
        P("pipe", None, None, None, None),
    )
    return jax.shard_map(
        on_device, mesh=mesh, in_specs=in_specs, out_specs=out_specs, check_vma=False
    )
```

profile of v0, /device:TPU:2, one launch (start us, length us, event | category | flops | bytes accessed | tf_op | source)
XLA Modules:
  0.0 690.7 jit_solution(15321098489667302605)
XLA Ops:
  7.2 3.7 fusion.4
  12.5 1.8 collective-permute-done
  14.5 2.0 collective-permute-start.1
  16.5 12.2 %collective-permute-done.1 = bf16[256,1024]{1,0:T(8,128)(2,1)S(1)} collective-permute-done((bf16[256,1024]{1,0:T(8,128)(2,1)S(1)}, bf16[256,1024]{1,0:T(8,128)(2,1)S(1)}, u32[]{:S(2)}, u32[]{:S(2)}) %collective-permute-start.1) | collective-permute-done | bytes 524320 | tf_op jit(solution)/shard_map/ppermute | solution.py:14
  28.9 3.4 collective-permute-start.2
  32.3 22.8 %collective-permute-done.2 = bf16[256,1024]{1,0:T(8,128)(2,1)S(1)} collective-permute-done((bf16[256,1024]{1,0:T(8,128)(2,1)S(1)}, bf16[256,1024]{1,0:T(8,128)(2,1)S(1)}, u32[]{:S(2)}, u32[]{:S(2)}) %collective-permute-start.2) | collective-permute-done | bytes 524320 | tf_op jit(solution)/shard_map/ppermute | solution.py:14
  55.3 6.3 collective-permute-start.3
  61.6 23.0 %collective-permute-done.3 = bf16[256,1024]{1,0:T(8,128)(2,1)S(1)} collective-permute-done((bf16[256,1024]{1,0:T(8,128)(2,1)S(1)}, bf16[256,1024]{1,0:T(8,128)(2,1)S(1)}, u32[]{:S(2)}, u32[]{:S(2)}) %collective-permute-start.3) | collective-permute-done | bytes 524320 | tf_op jit(solution)/shard_map/ppermute | solution.py:14
  84.8 1.7 collective-permute-start.4
  86.5 11.2 %collective-permute-done.4 = bf16[256,1024]{1,0:T(8,128)(2,1)S(1)} collective-permute-done((bf16[256,1024]{1,0:T(8,128)(2,1)S(1)}, bf16[256,1024]{1,0:T(8,128)(2,1)S(1)}, u32[]{:S(2)}, u32[]{:S(2)}) %collective-permute-start.4) | collective-permute-done | bytes 524320 | tf_op jit(solution)/shard_map/ppermute | solution.py:14
  97.9 3.3 collective-permute-start.5
  101.9 9.5 %collective-permute-done.5 = bf16[256,1024]{1,0:T(8,128)(2,1)S(1)} collective-permute-done((bf16[256,1024]{1,0:T(8,128)(2,1)S(1)}, bf16[256,1024]{1,0:T(8,128)(2,1)S(1)}, u32[]{:S(2)}, u32[]{:S(2)}) %collective-permute-start.5) | collective-permute-done | bytes 524320 | tf_op jit(solution)/shard_map/ppermute | solution.py:14
  112.8 3.2 collective-permute-start.6
  116.0 9.3 %collective-permute-done.6 = bf16[256,1024]{1,0:T(8,128)(2,1)S(1)} collective-permute-done((bf16[256,1024]{1,0:T(8,128)(2,1)S(1)}, bf16[256,1024]{1,0:T(8,128)(2,1)S(1)}, u32[]{:S(2)}, u32[]{:S(2)}) %collective-permute-start.6) | collective-permute-done | bytes 524320 | tf_op jit(solution)/shard_map/ppermute | solution.py:14
  125.8 1.7 collective-permute-start.7
  127.4 9.4 %collective-permute-done.7 = bf16[256,1024]{1,0:T(8,128)(2,1)S(1)} collective-permute-done((bf16[256,1024]{1,0:T(8,128)(2,1)S(1)}, bf16[256,1024]{1,0:T(8,128)(2,1)S(1)}, u32[]{:S(2)}, u32[]{:S(2)}) %collective-permute-start.7) | collective-permute-done | bytes 524320 | tf_op jit(solution)/shard_map/ppermute | solution.py:14
  137.3 2.0 collective-permute-start.8
  139.3 19.1 %collective-permute-done.8 = bf16[256,1024]{1,0:T(8,128)(2,1)S(1)} collective-permute-done((bf16[256,1024]{1,0:T(8,128)(2,1)S(1)}, bf16[256,1024]{1,0:T(8,128)(2,1)S(1)}, u32[]{:S(2)}, u32[]{:S(2)}) %collective-permute-start.8) | collective-permute-done | bytes 524320 | tf_op jit(solution)/shard_map/ppermute | solution.py:14
  159.0 18.6 %collective-permute-done.9 = bf16[256,1024]{1,0:T(8,128)(2,1)S(1)} collective-permute-done((bf16[256,1024]{1,0:T(8,128)(2,1)S(1)}, bf16[256,1024]{1,0:T(8,128)(2,1)S(1)}, u32[]{:S(2)}, u32[]{:S(2)}) %collective-permute-start.9) | collective-permute-done | bytes 524320 | tf_op jit(solution)/shard_map/ppermute | solution.py:14
  178.1 1.6 collective-permute-start.10
  179.7 12.5 %collective-permute-done.10 = bf16[256,1024]{1,0:T(8,128)(2,1)S(1)} collective-permute-done((bf16[256,1024]{1,0:T(8,128)(2,1)S(1)}, bf16[256,1024]{1,0:T(8,128)(2,1)S(1)}, u32[]{:S(2)}, u32[]{:S(2)}) %collective-permute-start.10) | collective-permute-done | bytes 524320 | tf_op jit(solution)/shard_map/ppermute | solution.py:14
  192.8 1.9 collective-permute-done.11
  195.1 4.5 convolution_bitcast_fusion
  199.6 9.2 %copy.17 = f32[1024,2048]{1,0:T(8,128)} copy(f32[1024,2048]{0,1:T(8,128)} %convolution_bitcast_fusion) | data formatting | bytes 16777216
  210.0 3.9 fusion.64
  214.0 3.8 fusion.17
  217.9 2.6 collective-permute-start.12
  223.1 10.9 %collective-permute-done.12 = bf16[256,1024]{1,0:T(8,128)(2,1)} collective-permute-done((bf16[256,1024]{1,0:T(8,128)(2,1)S(1)}, bf16[256,1024]{1,0:T(8,128)(2,1)}, u32[]{:S(2)}, u32[]{:S(2)}) %collective-permute-start.12) | collective-permute-done | bytes 524320 | tf_op jit(solution)/shard_map/ppermute | solution.py:20
  234.0 126.0 %reduce-scatter.7.cloned.1.call-done = f32[16,2048]{1,0:T(8,128)} async-done(((f32[1024,2048]{1,0:T(8,128)}), f32[16,2048]{1,0:T(8,128)}) %reduce-scatter.7.cloned.1.call-update) | async-done | bytes 131088
  362.2 172.9 %all-reduce.14.cloned.1.call-done = f32[1,6,2,2,1024]{4,3,2,1,0:T(2,128)} async-done(((f32[1,6,2,2,1024]{4,3,2,1,0:T(2,128)}), f32[1,6,2,2,1024]{4,3,2,1,0:T(2,128)}) %all-reduce.14.cloned.1.call-update) | async-done | bytes 98320 | tf_op jit(solution)/shard_map/psum | solution.py:85
  535.0 145.7 %reduce-scatter.5.cloned.1.call-done = f32[16,1024]{1,0:T(8,128)} async-done(((f32[1024,1024]{1,0:T(8,128)}), f32[16,1024]{1,0:T(8,128)}) %reduce-scatter.5.cloned.1.call-update) | async-done | bytes 65552 | tf_op jit(solution)/shard_map/reduce_scatter | solution.py:98
  680.8 1.9 copy.26
  (83 shorter events, 15.0 us)
Async XLA Ops:
  7.2 94.0 %copy-start = (bf16[1,1024,1024]{2,1,0:T(8,128)(2,1)S(1)}, bf16[1,1024,1024]{2,1,0:T(8,128)(2,1)}, u32[]{:S(2)}) copy-start(bf16[1,1024,1024]{2,1,0:T(8,128)(2,1)} %param.9) | copy-start | bytes 6291460
  7.2 4.8 copy-start.13
  7.2 5.2 copy-start.11
  7.2 352.8 %reduce-scatter.7.cloned.1.call-start = ((), (), s32[]{:S(2)}) async-start(), calls=%async_computation.4 | async-start | bytes 8519680
  11.0 1.0 copy-start.1
  12.3 2.0 collective-permute-start
  14.5 14.2 %collective-permute-start.1 = (bf16[256,1024]{1,0:T(8,128)(2,1)S(1)}, bf16[256,1024]{1,0:T(8,128)(2,1)S(1)}, u32[]{:S(2)}, u32[]{:S(2)}) collective-permute-start(bf16[256,1024]{1,0:T(8,128)(2,1)S(1)} %fusion.26), channel_id=1, source_target_pairs={{0,2},{2,0},{1,3},{3,1},{4,6},{6,4},{5,7},{7,5},{8,10},{10,8},{9,1... | collective-permute-start | bytes 1572872 | tf_op jit(solution)/shard_map/ppermute | solution.py:14
  28.9 26.1 %collective-permute-start.2 = (bf16[256,1024]{1,0:T(8,128)(2,1)S(1)}, bf16[256,1024]{1,0:T(8,128)(2,1)S(1)}, u32[]{:S(2)}, u32[]{:S(2)}) collective-permute-start(bf16[256,1024]{1,0:T(8,128)(2,1)S(1)} %fusion.28), channel_id=1, source_target_pairs={{0,4},{4,0},{1,5},{5,1},{2,6},{6,2},{3,7},{7,3},{8,12},{12,8},{9,1... | collective-permute-start | bytes 1572872 | tf_op jit(solution)/shard_map/ppermute | solution.py:14
  55.1 46.1 %copy-start.10 = (bf16[1,256,1024]{2,1,0:T(8,128)(2,1)S(1)}, bf16[1,256,1024]{2,1,0:T(8,128)(2,1)}, u32[]{:S(2)}) copy-start(bf16[1,256,1024]{2,1,0:T(8,128)(2,1)} %param.7) | copy-start | bytes 1572868
  55.3 29.3 %collective-permute-start.3 = (bf16[256,1024]{1,0:T(8,128)(2,1)S(1)}, bf16[256,1024]{1,0:T(8,128)(2,1)S(1)}, u32[]{:S(2)}, u32[]{:S(2)}) collective-permute-start(bf16[256,1024]{1,0:T(8,128)(2,1)S(1)} %fusion.30), channel_id=1, source_target_pairs={{0,8},{8,0},{1,9},{9,1},{2,10},{10,2},{3,11},{11,3},{4,12},{12,4},... | collective-permute-start | bytes 1572872 | tf_op jit(solution)/shard_map/ppermute | solution.py:14
  84.8 12.8 %collective-permute-start.4 = (bf16[256,1024]{1,0:T(8,128)(2,1)S(1)}, bf16[256,1024]{1,0:T(8,128)(2,1)S(1)}, u32[]{:S(2)}, u32[]{:S(2)}) collective-permute-start(bf16[256,1024]{1,0:T(8,128)(2,1)S(1)} %fusion.32), channel_id=1, source_target_pairs={{0,16},{16,0},{1,17},{17,1},{2,18},{18,2},{3,19},{19,3},{4,20},{20... | collective-permute-start | bytes 1572872 | tf_op jit(solution)/shard_map/ppermute | solution.py:14
  97.9 13.5 %copy-start.2 = (bf16[256,2048]{1,0:T(8,128)(2,1)S(1)}, bf16[256,2048]{1,0:T(8,128)(2,1)}, u32[]{:S(2)}) copy-start(bf16[256,2048]{1,0:T(8,128)(2,1)} %copy-done.1) | copy-start | bytes 3145732
  97.9 13.5 %collective-permute-start.5 = (bf16[256,1024]{1,0:T(8,128)(2,1)S(1)}, bf16[256,1024]{1,0:T(8,128)(2,1)S(1)}, u32[]{:S(2)}, u32[]{:S(2)}) collective-permute-start(bf16[256,1024]{1,0:T(8,128)(2,1)S(1)} %fusion.34), channel_id=1, source_target_pairs={{0,32},{32,0},{1,33},{33,1},{2,34},{34,2},{3,35},{35,3},{4,36},{36... | collective-permute-start | bytes 1572872 | tf_op jit(solution)/shard_map/ppermute | solution.py:14
  112.8 82.3 %copy-start.4 = (bf16[256,1024]{1,0:T(8,128)(2,1)}, bf16[256,1024]{1,0:T(8,128)(2,1)S(1)}, u32[]{:S(2)}) copy-start(bf16[256,1024]{1,0:T(8,128)(2,1)S(1)} %get-tuple-element.38) | copy-start | bytes 1572868
  112.8 12.6 %collective-permute-start.6 = (bf16[256,1024]{1,0:T(8,128)(2,1)S(1)}, bf16[256,1024]{1,0:T(8,128)(2,1)S(1)}, u32[]{:S(2)}, u32[]{:S(2)}) collective-permute-start(bf16[256,1024]{1,0:T(8,128)(2,1)S(1)} %get-tuple-element.30), channel_id=1, source_target_pairs={{0,32},{32,0},{1,33},{33,1},{2,34},{34,2},{3,35},{35,3},{4,36},{36... | collective-permute-start | bytes 1572872 | tf_op jit(solution)/shard_map/ppermute | solution.py:14
  125.8 11.1 %collective-permute-start.7 = (bf16[256,1024]{1,0:T(8,128)(2,1)S(1)}, bf16[256,1024]{1,0:T(8,128)(2,1)S(1)}, u32[]{:S(2)}, u32[]{:S(2)}) collective-permute-start(bf16[256,1024]{1,0:T(8,128)(2,1)S(1)} %get-tuple-element.31), channel_id=1, source_target_pairs={{0,16},{16,0},{1,17},{17,1},{2,18},{18,2},{3,19},{19,3},{4,20},{20... | collective-permute-start | bytes 1572872 | tf_op jit(solution)/shard_map/ppermute | solution.py:14
  137.3 21.1 %collective-permute-start.8 = (bf16[256,1024]{1,0:T(8,128)(2,1)S(1)}, bf16[256,1024]{1,0:T(8,128)(2,1)S(1)}, u32[]{:S(2)}, u32[]{:S(2)}) collective-permute-start(bf16[256,1024]{1,0:T(8,128)(2,1)S(1)} %get-tuple-element.32), channel_id=1, source_target_pairs={{0,8},{8,0},{1,9},{9,1},{2,10},{10,2},{3,11},{11,3},{4,12},{12,4},... | collective-permute-start | bytes 1572872 | tf_op jit(solution)/shard_map/ppermute | solution.py:14
  158.9 18.7 %collective-permute-start.9 = (bf16[256,1024]{1,0:T(8,128)(2,1)S(1)}, bf16[256,1024]{1,0:T(8,128)(2,1)S(1)}, u32[]{:S(2)}, u32[]{:S(2)}) collective-permute-start(bf16[256,1024]{1,0:T(8,128)(2,1)S(1)} %get-tuple-element.33), channel_id=1, source_target_pairs={{0,4},{4,0},{1,5},{5,1},{2,6},{6,2},{3,7},{7,3},{8,12},{12,8},{9,1... | collective-permute-start | bytes 1572872 | tf_op jit(solution)/shard_map/ppermute | solution.py:14
  178.1 14.1 %collective-permute-start.10 = (bf16[256,1024]{1,0:T(8,128)(2,1)S(1)}, bf16[256,1024]{1,0:T(8,128)(2,1)S(1)}, u32[]{:S(2)}, u32[]{:S(2)}) collective-permute-start(bf16[256,1024]{1,0:T(8,128)(2,1)S(1)} %get-tuple-element.34), channel_id=1, source_target_pairs={{0,2},{2,0},{1,3},{3,1},{4,6},{6,4},{5,7},{7,5},{8,10},{10,8},{9,1... | collective-permute-start | bytes 1572872 | tf_op jit(solution)/shard_map/ppermute | solution.py:14
  192.2 2.9 copy-start.6
  192.6 2.0 copy-start.7
  192.6 2.0 collective-permute-start.11
  194.6 5.0 copy-start.14
  195.1 4.5 copy-start.9
  208.8 1.2 copy-start.3
  208.8 326.2 %all-reduce.14.cloned.1.call-start = ((), (), s32[]{:S(2)}) async-start(), calls=%async_computation.3 | async-start | bytes 196608 | tf_op jit(solution)/shard_map/psum | solution.py:85
  209.1 0.6 copy-start.12
  209.8 470.9 %reduce-scatter.5.cloned.1.call-start = ((), (), s32[]{:S(2)}) async-start(), calls=%async_computation.2 | async-start | bytes 4259840 | tf_op jit(solution)/shard_map/reduce_scatter | solution.py:98
  214.0 6.5 copy-start.5
  217.9 4.1 copy-start.8
  217.9 4.1 copy-start.15
  217.9 16.1 %collective-permute-start.12 = (bf16[256,1024]{1,0:T(8,128)(2,1)S(1)}, bf16[256,1024]{1,0:T(8,128)(2,1)}, u32[]{:S(2)}, u32[]{:S(2)}) collective-permute-start(bf16[256,1024]{1,0:T(8,128)(2,1)S(1)} %fusion.17), channel_id=1, source_target_pairs={{64,0},{128,64},{192,128},{65,1},{129,65},{193,129},{66,2},{130,66... | collective-permute-start | bytes 1572872 | tf_op jit(solution)/shard_map/ppermute | solution.py:20
Sparse Core Ops, SparseCore 0:
  209.0 150.9 reduce-scatter.6
  364.0 170.9 all-reduce.13
  539.8 140.9 reduce-scatter.4
where the time goes:
time: 691 us
  waiting for transfers between devices  607 us (88%)
  starting transfers between devices  28 us (4%)
  matrix products  20.1 us (3%)
  local copies, waits for them, and re-layouts  16.7 us (2%)
  between operations  14.1 us (2%)
    psum x1, waiting for transfers between devices, on_device(): twiddle_grad = lax.psum(jnp.stack(partials), 'seq')  173 us
    ppermute x12, waiting for transfers between devices, swapped(): return lax.ppermute(block, axis, route)  151 us
    reduce_scatter x1, waiting for transfers between devices, on_device(): lax.psum_scatter(wout_term, 'seq', scatter_dimension=0, tiled=True)  146 us
    unnamed x4, waiting for transfers between devices  126 us
    ppermute x12, starting transfers between devices, swapped(): return lax.ppermute(block, axis, route)  25.3 us
    unnamed x37, local copies, waits for them, and re-layouts  16.7 us
  transfers between devices with their start and end apart: 16, of which 16 were waited for; matrix products, arithmetic and copies ran while one was open for 2% of the time, Pallas kernels for 0%

commit v1 on v0

--- a/solution.py
+++ b/solution.py
@@ -1,7 +1,16 @@
+import functools
 import jax
 import jax.numpy as jnp
 from jax import lax
 from jax.sharding import PartitionSpec as P
+
+
+def work_zone_for(v0, across):
+    piece_out = jax.lax.all_gather(v0, axis_name=across)
+    return jnp.sum(piece_out, axis=0)
+
+
+store_sums_all_by_axis = functools.partial(work_zone_for, across="seq")
 
 
 def swapped(block, axis, apart):
@@ -82,7 +91,7 @@
         grad_now = (
             own_coef[0] * grad_float + peer_coef[1] * grad_partner.astype(jnp.float32)
         ).astype(jnp.bfloat16)
-    twiddle_grad = lax.psum(jnp.stack(partials), "seq")
+    twiddle_grad = store_sums_all_by_axis(jnp.stack(partials))
     d_value = lax.dot_general(
         square_mix, grad_now, (((0,), (0,)), ((), ())), preferred_element_type=jnp.float32
     ).astype(jnp.bfloat16)

time: 691 us -> 583 us (0.84)
  waiting for transfers between devices: 607 us -> 490 us
  other arithmetic: 4.89 us -> 12.4 us
    psum x1 -> x0, waiting for transfers between devices: 173 us -> none  [on_device(): twiddle_grad = lax.psum(jnp.stack(partials), 'seq')]
    all_gather x0 -> x1, waiting for transfers between devices: none -> 35.6 us  [work_zone_for(): piece_out = jax.lax.all_gather(v0, axis_name=across)]
    unnamed x4, waiting for transfers between devices: 126 us -> 147 us
    unnamed x37 -> x34, local copies, waits for them, and re-layouts: 16.7 us -> 16.9 us
  transfers between devices with their start and end apart: 16 -> 16, of which waited for: 16 -> 16; matrix products, arithmetic and copies ran while one was open for 2% -> 6% of each run, Pallas kernels for 0% -> 0%
where the time goes in v1:
time: 583 us
  waiting for transfers between devices  490 us (84%)
  starting transfers between devices  28 us (5%)
  matrix products  21.3 us (4%)
  local copies, waits for them, and re-layouts  16.9 us (3%)
  between operations  14.1 us (2%)
  other arithmetic  12.4 us (2%)
    ppermute x12, waiting for transfers between devices, swapped(): return lax.ppermute(block, axis, route)  151 us
    unnamed x4, waiting for transfers between devices  147 us
    reduce_scatter x1, waiting for transfers between devices, on_device(): lax.psum_scatter(wout_term, 'seq', scatter_dimension=0, tiled=True)  145 us
    all_gather x1, waiting for transfers between devices, work_zone_for(): piece_out = jax.lax.all_gather(v0, axis_name=across)  35.6 us
    ppermute x12, starting transfers between devices, swapped(): return lax.ppermute(block, axis, route)  25.3 us
    unnamed x34, local copies, waits for them, and re-layouts  16.9 us
  transfers between devices with their start and end apart: 16, of which 16 were waited for; matrix products, arithmetic and copies ran while one was open for 6% of the time, Pallas kernels for 0%

profile of v1, /device:TPU:2, one launch (start us, length us, event | category | flops | bytes accessed | tf_op | source)
XLA Modules:
  0.0 582.7 jit_solution(9527424359201713282)
XLA Ops:
  7.2 3.7 fusion.4
  12.5 1.8 collective-permute-done
  14.5 2.0 collective-permute-start.1
  16.5 12.2 %collective-permute-done.1 = bf16[256,1024]{1,0:T(8,128)(2,1)S(1)} collective-permute-done((bf16[256,1024]{1,0:T(8,128)(2,1)S(1)}, bf16[256,1024]{1,0:T(8,128)(2,1)S(1)}, u32[]{:S(2)}, u32[]{:S(2)}) %collective-permute-start.1) | collective-permute-done | bytes 524320 | tf_op jit(solution)/shard_map/ppermute | solution.py:23
  29.0 3.4 collective-permute-start.2
  32.3 22.8 %collective-permute-done.2 = bf16[256,1024]{1,0:T(8,128)(2,1)S(1)} collective-permute-done((bf16[256,1024]{1,0:T(8,128)(2,1)S(1)}, bf16[256,1024]{1,0:T(8,128)(2,1)S(1)}, u32[]{:S(2)}, u32[]{:S(2)}) %collective-permute-start.2) | collective-permute-done | bytes 524320 | tf_op jit(solution)/shard_map/ppermute | solution.py:23
  55.3 6.3 %collective-permute-start.3 = (bf16[256,1024]{1,0:T(8,128)(2,1)S(1)}, bf16[256,1024]{1,0:T(8,128)(2,1)S(1)}, u32[]{:S(2)}, u32[]{:S(2)}) collective-permute-start(bf16[256,1024]{1,0:T(8,128)(2,1)S(1)} %fusion.30), channel_id=1, source_target_pairs={{0,8},{8,0},{1,9},{9,1},{2,10},{10,2},{3,11},{11,3},{4,12},{12,4},... | collective-permute-start | bytes 1572872 | tf_op jit(solution)/shard_map/ppermute | solution.py:23
  61.6 23.0 %collective-permute-done.3 = bf16[256,1024]{1,0:T(8,128)(2,1)S(1)} collective-permute-done((bf16[256,1024]{1,0:T(8,128)(2,1)S(1)}, bf16[256,1024]{1,0:T(8,128)(2,1)S(1)}, u32[]{:S(2)}, u32[]{:S(2)}) %collective-permute-start.3) | collective-permute-done | bytes 524320 | tf_op jit(solution)/shard_map/ppermute | solution.py:23
  84.9 1.7 collective-permute-start.4
  86.5 11.2 %collective-permute-done.4 = bf16[256,1024]{1,0:T(8,128)(2,1)S(1)} collective-permute-done((bf16[256,1024]{1,0:T(8,128)(2,1)S(1)}, bf16[256,1024]{1,0:T(8,128)(2,1)S(1)}, u32[]{:S(2)}, u32[]{:S(2)}) %collective-permute-start.4) | collective-permute-done | bytes 524320 | tf_op jit(solution)/shard_map/ppermute | solution.py:23
  97.9 3.3 collective-permute-start.5
  102.0 9.5 %collective-permute-done.5 = bf16[256,1024]{1,0:T(8,128)(2,1)S(1)} collective-permute-done((bf16[256,1024]{1,0:T(8,128)(2,1)S(1)}, bf16[256,1024]{1,0:T(8,128)(2,1)S(1)}, u32[]{:S(2)}, u32[]{:S(2)}) %collective-permute-start.5) | collective-permute-done | bytes 524320 | tf_op jit(solution)/shard_map/ppermute | solution.py:23
  112.9 3.2 collective-permute-start.6
  116.2 9.3 %collective-permute-done.6 = bf16[256,1024]{1,0:T(8,128)(2,1)S(1)} collective-permute-done((bf16[256,1024]{1,0:T(8,128)(2,1)S(1)}, bf16[256,1024]{1,0:T(8,128)(2,1)S(1)}, u32[]{:S(2)}, u32[]{:S(2)}) %collective-permute-start.6) | collective-permute-done | bytes 524320 | tf_op jit(solution)/shard_map/ppermute | solution.py:23
  125.9 1.7 collective-permute-start.7
  127.6 9.5 %collective-permute-done.7 = bf16[256,1024]{1,0:T(8,128)(2,1)S(1)} collective-permute-done((bf16[256,1024]{1,0:T(8,128)(2,1)S(1)}, bf16[256,1024]{1,0:T(8,128)(2,1)S(1)}, u32[]{:S(2)}, u32[]{:S(2)}) %collective-permute-start.7) | collective-permute-done | bytes 524320 | tf_op jit(solution)/shard_map/ppermute | solution.py:23
  137.5 2.0 collective-permute-start.8
  139.5 19.1 %collective-permute-done.8 = bf16[256,1024]{1,0:T(8,128)(2,1)S(1)} collective-permute-done((bf16[256,1024]{1,0:T(8,128)(2,1)S(1)}, bf16[256,1024]{1,0:T(8,128)(2,1)S(1)}, u32[]{:S(2)}, u32[]{:S(2)}) %collective-permute-start.8) | collective-permute-done | bytes 524320 | tf_op jit(solution)/shard_map/ppermute | solution.py:23
  159.2 18.6 %collective-permute-done.9 = bf16[256,1024]{1,0:T(8,128)(2,1)S(1)} collective-permute-done((bf16[256,1024]{1,0:T(8,128)(2,1)S(1)}, bf16[256,1024]{1,0:T(8,128)(2,1)S(1)}, u32[]{:S(2)}, u32[]{:S(2)}) %collective-permute-start.9) | collective-permute-done | bytes 524320 | tf_op jit(solution)/shard_map/ppermute | solution.py:23
  180.0 12.4 %collective-permute-done.10 = bf16[256,1024]{1,0:T(8,128)(2,1)S(1)} collective-permute-done((bf16[256,1024]{1,0:T(8,128)(2,1)S(1)}, bf16[256,1024]{1,0:T(8,128)(2,1)S(1)}, u32[]{:S(2)}, u32[]{:S(2)}) %collective-permute-start.10) | collective-permute-done | bytes 524320 | tf_op jit(solution)/shard_map/ppermute | solution.py:23
  194.5 2.1 collective-permute-done.11
  199.1 4.5 convolution_bitcast_fusion
  203.6 9.2 %copy.17 = f32[1024,2048]{1,0:T(8,128)} copy(f32[1024,2048]{0,1:T(8,128)} %convolution_bitcast_fusion) | data formatting | bytes 16777216
  214.0 3.9 fusion.64
  218.0 3.9 fusion.17
  221.9 2.6 collective-permute-start.12
  227.1 10.9 %collective-permute-done.12 = bf16[256,1024]{1,0:T(8,128)(2,1)} collective-permute-done((bf16[256,1024]{1,0:T(8,128)(2,1)S(1)}, bf16[256,1024]{1,0:T(8,128)(2,1)}, u32[]{:S(2)}, u32[]{:S(2)}) %collective-permute-start.12) | collective-permute-done | bytes 524320 | tf_op jit(solution)/shard_map/ppermute | solution.py:29
  238.0 35.6 %all-gather.3.cloned.1.call-done = f32[384,2,2,1024]{3,2,1,0:T(2,128)} async-done(((f32[6,2,2,1024]{3,2,1,0:T(2,128)}), f32[384,2,2,1024]{3,2,1,0:T(2,128)}) %all-gather.3.cloned.1.call-update) | async-done | bytes 6291472 | tf_op jit(solution)/shard_map/all_gather | solution.py:9
  273.6 6.6 %reduce_sum.129 = f32[6,2,2,1024]{3,2,1,0:T(2,128)} reduce(f32[64,6,2,2,1024]{4,3,2,1,0:T(2,128)} %bitcast.106, f32[]{:T(128)} %constant.6.clone.1), dimensions={0}, to_apply=%region_14.15 | reduce | flops 1548288 | bytes 6389764 | tf_op jit(solution)/shard_map/reduce_sum | solution.py:10
  280.1 146.8 %reduce-scatter.7.cloned.1.call-done = f32[16,2048]{1,0:T(8,128)} async-done(((f32[1024,2048]{1,0:T(8,128)}), f32[16,2048]{1,0:T(8,128)}) %reduce-scatter.7.cloned.1.call-update) | async-done | bytes 131088
  429.1 145.2 %reduce-scatter.5.cloned.1.call-done = f32[16,1024]{1,0:T(8,128)} async-done(((f32[1024,1024]{1,0:T(8,128)}), f32[16,1024]{1,0:T(8,128)}) %reduce-scatter.5.cloned.1.call-update) | async-done | bytes 65552 | tf_op jit(solution)/shard_map/reduce_scatter | solution.py:107
  574.3 1.9 copy.25
  (81 shorter events, 19.0 us)
Async XLA Ops:
  7.2 94.0 %copy-start = (bf16[1,1024,1024]{2,1,0:T(8,128)(2,1)S(1)}, bf16[1,1024,1024]{2,1,0:T(8,128)(2,1)}, u32[]{:S(2)}) copy-start(bf16[1,1024,1024]{2,1,0:T(8,128)(2,1)} %param.9) | copy-start | bytes 6291460
  7.2 4.8 copy-start.12
  7.2 5.2 copy-start.10
  7.2 266.4 %all-gather.3.cloned.1.call-start = ((), (), s32[]{:S(2)}) async-start(), calls=%async_computation.3 | async-start | bytes 6389760 | tf_op jit(solution)/shard_map/all_gather | solution.py:9
  11.0 1.0 copy-start.1
  12.3 2.0 collective-permute-start
  14.5 14.2 %collective-permute-start.1 = (bf16[256,1024]{1,0:T(8,128)(2,1)S(1)}, bf16[256,1024]{1,0:T(8,128)(2,1)S(1)}, u32[]{:S(2)}, u32[]{:S(2)}) collective-permute-start(bf16[256,1024]{1,0:T(8,128)(2,1)S(1)} %fusion.26), channel_id=1, source_target_pairs={{0,2},{2,0},{1,3},{3,1},{4,6},{6,4},{5,7},{7,5},{8,10},{10,8},{9,1... | collective-permute-start | bytes 1572872 | tf_op jit(solution)/shard_map/ppermute | solution.py:23
  29.0 26.1 %collective-permute-start.2 = (bf16[256,1024]{1,0:T(8,128)(2,1)S(1)}, bf16[256,1024]{1,0:T(8,128)(2,1)S(1)}, u32[]{:S(2)}, u32[]{:S(2)}) collective-permute-start(bf16[256,1024]{1,0:T(8,128)(2,1)S(1)} %fusion.28), channel_id=1, source_target_pairs={{0,4},{4,0},{1,5},{5,1},{2,6},{6,2},{3,7},{7,3},{8,12},{12,8},{9,1... | collective-permute-start | bytes 1572872 | tf_op jit(solution)/shard_map/ppermute | solution.py:23
  55.1 46.1 %copy-start.9 = (bf16[1,256,1024]{2,1,0:T(8,128)(2,1)S(1)}, bf16[1,256,1024]{2,1,0:T(8,128)(2,1)}, u32[]{:S(2)}) copy-start(bf16[1,256,1024]{2,1,0:T(8,128)(2,1)} %param.7) | copy-start | bytes 1572868
  55.3 29.3 %collective-permute-start.3 = (bf16[256,1024]{1,0:T(8,128)(2,1)S(1)}, bf16[256,1024]{1,0:T(8,128)(2,1)S(1)}, u32[]{:S(2)}, u32[]{:S(2)}) collective-permute-start(bf16[256,1024]{1,0:T(8,128)(2,1)S(1)} %fusion.30), channel_id=1, source_target_pairs={{0,8},{8,0},{1,9},{9,1},{2,10},{10,2},{3,11},{11,3},{4,12},{12,4},... | collective-permute-start | bytes 1572872 | tf_op jit(solution)/shard_map/ppermute | solution.py:23
  84.9 12.8 %collective-permute-start.4 = (bf16[256,1024]{1,0:T(8,128)(2,1)S(1)}, bf16[256,1024]{1,0:T(8,128)(2,1)S(1)}, u32[]{:S(2)}, u32[]{:S(2)}) collective-permute-start(bf16[256,1024]{1,0:T(8,128)(2,1)S(1)} %fusion.32), channel_id=1, source_target_pairs={{0,16},{16,0},{1,17},{17,1},{2,18},{18,2},{3,19},{19,3},{4,20},{20... | collective-permute-start | bytes 1572872 | tf_op jit(solution)/shard_map/ppermute | solution.py:23
  97.9 13.5 %copy-start.2 = (bf16[256,2048]{1,0:T(8,128)(2,1)S(1)}, bf16[256,2048]{1,0:T(8,128)(2,1)}, u32[]{:S(2)}) copy-start(bf16[256,2048]{1,0:T(8,128)(2,1)} %copy-done.1) | copy-start | bytes 3145732
  97.9 13.5 %collective-permute-start.5 = (bf16[256,1024]{1,0:T(8,128)(2,1)S(1)}, bf16[256,1024]{1,0:T(8,128)(2,1)S(1)}, u32[]{:S(2)}, u32[]{:S(2)}) collective-permute-start(bf16[256,1024]{1,0:T(8,128)(2,1)S(1)} %fusion.34), channel_id=1, source_target_pairs={{0,32},{32,0},{1,33},{33,1},{2,34},{34,2},{3,35},{35,3},{4,36},{36... | collective-permute-start | bytes 1572872 | tf_op jit(solution)/shard_map/ppermute | solution.py:23
  112.9 12.6 %collective-permute-start.6 = (bf16[256,1024]{1,0:T(8,128)(2,1)S(1)}, bf16[256,1024]{1,0:T(8,128)(2,1)S(1)}, u32[]{:S(2)}, u32[]{:S(2)}) collective-permute-start(bf16[256,1024]{1,0:T(8,128)(2,1)S(1)} %get-tuple-element.30), channel_id=1, source_target_pairs={{0,32},{32,0},{1,33},{33,1},{2,34},{34,2},{3,35},{35,3},{4,36},{36... | collective-permute-start | bytes 1572872 | tf_op jit(solution)/shard_map/ppermute | solution.py:23
  125.9 11.1 %collective-permute-start.7 = (bf16[256,1024]{1,0:T(8,128)(2,1)S(1)}, bf16[256,1024]{1,0:T(8,128)(2,1)S(1)}, u32[]{:S(2)}, u32[]{:S(2)}) collective-permute-start(bf16[256,1024]{1,0:T(8,128)(2,1)S(1)} %get-tuple-element.31), channel_id=1, source_target_pairs={{0,16},{16,0},{1,17},{17,1},{2,18},{18,2},{3,19},{19,3},{4,20},{20... | collective-permute-start | bytes 1572872 | tf_op jit(solution)/shard_map/ppermute | solution.py:23
  137.5 21.1 %collective-permute-start.8 = (bf16[256,1024]{1,0:T(8,128)(2,1)S(1)}, bf16[256,1024]{1,0:T(8,128)(2,1)S(1)}, u32[]{:S(2)}, u32[]{:S(2)}) collective-permute-start(bf16[256,1024]{1,0:T(8,128)(2,1)S(1)} %get-tuple-element.32), channel_id=1, source_target_pairs={{0,8},{8,0},{1,9},{9,1},{2,10},{10,2},{3,11},{11,3},{4,12},{12,4},... | collective-permute-start | bytes 1572872 | tf_op jit(solution)/shard_map/ppermute | solution.py:23
  159.0 18.8 %collective-permute-start.9 = (bf16[256,1024]{1,0:T(8,128)(2,1)S(1)}, bf16[256,1024]{1,0:T(8,128)(2,1)S(1)}, u32[]{:S(2)}, u32[]{:S(2)}) collective-permute-start(bf16[256,1024]{1,0:T(8,128)(2,1)S(1)} %get-tuple-element.33), channel_id=1, source_target_pairs={{0,4},{4,0},{1,5},{5,1},{2,6},{6,2},{3,7},{7,3},{8,12},{12,8},{9,1... | collective-permute-start | bytes 1572872 | tf_op jit(solution)/shard_map/ppermute | solution.py:23
  178.2 14.1 %collective-permute-start.10 = (bf16[256,1024]{1,0:T(8,128)(2,1)S(1)}, bf16[256,1024]{1,0:T(8,128)(2,1)S(1)}, u32[]{:S(2)}, u32[]{:S(2)}) collective-permute-start(bf16[256,1024]{1,0:T(8,128)(2,1)S(1)} %get-tuple-element.34), channel_id=1, source_target_pairs={{0,2},{2,0},{1,3},{3,1},{4,6},{6,4},{5,7},{7,5},{8,10},{10,8},{9,1... | collective-permute-start | bytes 1572872 | tf_op jit(solution)/shard_map/ppermute | solution.py:23
  193.6 5.5 copy-start.4
  193.6 5.5 copy-start.6
  193.7 0.6 copy-start.11
  194.4 232.6 %reduce-scatter.7.cloned.1.call-start = ((), (), s32[]{:S(2)}) async-start(), calls=%async_computation.4 | async-start | bytes 8519680
  194.4 2.2 collective-permute-start.11
  196.6 1.6 copy-start.13
  198.3 0.8 copy-start.8
  212.8 1.2 copy-start.3
  212.8 361.5 %reduce-scatter.5.cloned.1.call-start = ((), (), s32[]{:S(2)}) async-start(), calls=%async_computation.2 | async-start | bytes 4259840 | tf_op jit(solution)/shard_map/reduce_scatter | solution.py:107
  218.0 6.5 %copy-start.5 = (bf16[256,1024]{1,0:T(8,128)(2,1)S(1)}, bf16[256,1024]{1,0:T(8,128)(2,1)}, u32[]{:S(2)}) copy-start(bf16[256,1024]{1,0:T(8,128)(2,1)} %get-tuple-element.39) | copy-start | bytes 1572868
  221.9 4.1 copy-start.7
  221.9 4.1 copy-start.14
  221.9 16.1 %collective-permute-start.12 = (bf16[256,1024]{1,0:T(8,128)(2,1)S(1)}, bf16[256,1024]{1,0:T(8,128)(2,1)}, u32[]{:S(2)}, u32[]{:S(2)}) collective-permute-start(bf16[256,1024]{1,0:T(8,128)(2,1)S(1)} %fusion.17), channel_id=1, source_target_pairs={{64,0},{128,64},{192,128},{65,1},{129,65},{193,129},{66,2},{130,66... | collective-permute-start | bytes 1572872 | tf_op jit(solution)/shard_map/ppermute | solution.py:29
Sparse Core Ops, SparseCore 0:
  194.5 79.0 all-gather.2
  277.8 149.1 reduce-scatter.6
  431.6 142.6 reduce-scatter.4
